TPU v7x, 512 devices: a whole 4x8x8 slice. The times are simulated.
512 devices in a mesh: row: 16 (over x_lo, z), col: 32 (over y, x_hi, core).
Axes of the slice: x: 4 (x_hi: 2, x_lo: 2; x = x_hi * 2 + x_lo), y: 8, z: 8, core: 2. Of those that a mesh axis runs over, the one named last changes fastest.
Arguments:
- protocols: float32 [20, 65536], P(None, ('row', 'col')), may hold values from -6 to 6
- w_in: float32 [20, 256], replicated, may hold values from -1.25 to 1.25
- b_in: float32 [256], replicated, may hold values from -3 to 3
- w_out: float32 [256, 64], replicated, may hold values from -0.21875 to 0.21875
- solved: float32 [32, 65536], P(None, ('row', 'col')), may hold values from -0.5 to 0.5
- probes: float32 [32, 65536], P(None, ('row', 'col')), may hold values from -6 to 6
- window_blocks: int32 [16], replicated, may hold values from 0 to 31
Outputs:
- col_grad: float32 [64, 65536], P(None, ('row', 'col'))
- grad_in: float32 [20, 256], replicated
- grad_bias: float32 [256], replicated
- grad_out: float32 [256, 64], replicated
Inputs may be any that keep to these rules, and one draw needn't show every extreme that they name: Window block r is the 128 protocols held at index r of row and index window_blocks[r] of col.
All inputs are finite; a program needn't handle non-finite values.
Results may differ from a plain program's by a relative error of at most 0.0003.
Values sent between devices are 32-bit elements; how exact they have to be, the bound alone decides.
A program may use at most 64 MiB of HBM per device.

v0:
```python
import jax
import jax.numpy as jnp
from jax import lax
from jax.sharding import PartitionSpec as P

HIGHEST = lax.Precision.HIGHEST


def spread(value, axis, source):
    kept = jnp.where(lax.axis_index(axis) == source, value, 0).astype(value.dtype)
    return lax.psum(kept, axis)


def tile_pass(first_feat, first_vec, second_feat, second_vec):
    first_norm = jnp.sum(first_feat * first_feat, 0)
    second_norm = jnp.sum(second_feat * second_feat, 0)
    cross = jnp.einsum("fi,fj->ij", first_feat, second_feat, precision=HIGHEST)
    kern = jnp.exp(-0.5 * (first_norm[:, None] + second_norm[None, :] - 2.0 * cross))
    weigh = jnp.einsum("qi,qj->ij", first_vec, second_vec, precision=HIGHEST) * kern
    first_grad = (
        jnp.einsum("fj,ij->fi", second_feat, weigh, precision=HIGHEST)
        - first_feat * jnp.sum(weigh, 1)[None, :]
    )
    second_grad = (
        jnp.einsum("fi,ij->fj", first_feat, weigh, precision=HIGHEST)
        - second_feat * jnp.sum(weigh, 0)[None, :]
    )
    return (first_grad, second_grad)


def blocked(first_feat, first_vec, second_feat, second_vec):
    width = second_feat.shape[1]
    block_width = 1024
    count = width // block_width
    split_feat = second_feat.reshape(second_feat.shape[0], count, block_width).transpose(1, 0, 2)
    split_vec = second_vec.reshape(second_vec.shape[0], count, block_width).transpose(1, 0, 2)

    def partial_pass(running, pair):
        first_part, second_part = tile_pass(first_feat, first_vec, pair[0], pair[1])
        return (running + first_part, second_part)

    first_grad, second_parts = lax.scan(
        partial_pass, jnp.zeros_like(first_feat), (split_feat, split_vec)
    )
    return (first_grad, second_parts.transpose(1, 0, 2).reshape(second_feat.shape[0], width))


def hidden_of(w_in, b_in, inputs):
    return jnp.tanh(jnp.einsum("ph,pn->hn", w_in, inputs, precision=HIGHEST) + b_in[:, None])


def backprop(w_out, inputs, hidden, grads):
    grad_out = jnp.einsum("hn,fn->hf", hidden, grads, precision=HIGHEST)
    grad_hidden = jnp.einsum("hf,fn->hn", w_out, grads, precision=HIGHEST)
    grad_pre = grad_hidden * (1.0 - hidden * hidden)
    grad_in = jnp.einsum("pn,hn->ph", inputs, grad_pre, precision=HIGHEST)
    return (grad_in, jnp.sum(grad_pre, 1), grad_out)


def window_total(partial_grad):
    return lax.psum(partial_grad, "col")


def per_device(protocols, w_in, b_in, w_out, solved, probes, window_blocks):
    hidden = hidden_of(w_in, b_in, protocols)
    features = jnp.einsum("hf,hn->fn", w_out, hidden, precision=HIGHEST)
    owner_col = window_blocks[lax.axis_index("row")]
    is_owner = lax.axis_index("col") == owner_col
    window = (spread(features, "col", owner_col), spread(solved, "col", owner_col))
    win_part, col_part = blocked(
        window[0],
        window[1],
        lax.all_gather(features, "row", axis=1, tiled=True),
        lax.all_gather(probes, "row", axis=1, tiled=True),
    )
    col_grad = lax.psum_scatter(col_part, "row", scatter_dimension=1, tiled=True)
    summed = window_total(win_part)
    own_total = col_grad + jnp.where(is_owner, summed, jnp.zeros_like(summed))
    terms = backprop(w_out, protocols, hidden, own_total)
    grad_in, grad_bias, grad_out = lax.psum((terms[0], terms[1], terms[2]), ("row", "col"))
    return (col_grad, grad_in, grad_bias, grad_out)


def solution(mesh):
    in_specs = (
        P(None, ("row", "col")),
        P(),
        P(),
        P(),
        P(None, ("row", "col")),
        P(None, ("row", "col")),
        P(),
    )
    out_specs = (P(None, ("row", "col")), P(), P(), P())
    return jax.shard_map(
        per_device, mesh=mesh, in_specs=in_specs, out_specs=out_specs, check_vma=False
    )
```

profile of v0, /device:TPU:1, one launch (start us, length us, event | category | flops | bytes accessed | tf_op | source)
XLA Modules:
  0.0 622.4 jit_solution(2819054057416116378)
XLA Ops:
  7.2 0.0 copy-start
  7.2 0.0 copy-start.5
  7.2 0.0 reduce-scatter.2.cloned.1.call-start
  7.3 0.0 copy-start.7
  7.3 0.0 copy-start.3
  7.3 0.6 copy-done.7
  7.9 0.6 dynamic_slice.15
  9.2 0.0 copy-done.5
  9.2 0.0 copy-start.2
  9.2 0.0 copy-start.6
  9.2 0.0 copy-done.3
  9.2 0.7 copy-done.2
  9.9 0.0 copy-done.6
  9.9 0.3 fusion.17
  10.2 0.0 copy-done
  10.2 0.3 broadcast_select_fusion
  10.5 129.4 %all-reduce.1 = (f32[32,128]{1,0:T(8,128)S(1)}, f32[64,128]{1,0:T(8,128)S(1)}) all-reduce(f32[32,128]{1,0:T(8,128)S(1)} %broadcast_select_fusion.1, f32[64,128]{1,0:T(8,128)S(1)} %get-tuple-element.153), channel_id=1, replica_groups=mesh['row'=16,'col'=32] {'col'}, use_global_device_ids=true, to_apply=%region_1.2 | all-reduce | flops 12288 | bytes 98304 | tf_op jit(solution)/shard_map/psum | solution.py:11
  139.9 0.0 copy-start.4
  139.9 0.7 copy-done.4
  140.6 32.7 %all_gather.7 = f32[32,2048]{1,0:T(8,128)S(1)} all-gather(f32[32,128]{1,0:T(8,128)S(1)} %copy-done.4), channel_id=1, replica_groups=mesh['row'=16,'col'=32] {'row'}, dimensions={1}, use_global_device_ids=true | all-gather | bytes 278528 | tf_op jit(solution)/shard_map/all_gather | solution.py:74
  173.3 0.2 reshape.23
  173.5 26.2 %all_gather.6 = f32[64,2048]{1,0:T(8,128)S(1)} all-gather(f32[64,128]{1,0:T(8,128)S(1)} %get-tuple-element.154), channel_id=1, replica_groups=mesh['row'=16,'col'=32] {'row'}, dimensions={1}, use_global_device_ids=true | all-gather | bytes 557056 | tf_op jit(solution)/shard_map/all_gather | solution.py:73
  199.7 7.0 %while.15 = (s32[]{:T(128)}, f32[64,128]{1,0:T(8,128)S(1)}, f32[2,64,1024]{2,1,0:T(8,128)S(1)}, f32[2,64,1024]{2,1,0:T(8,128)S(1)}, f32[2,32,1024]{2,0,1:T(2,128...) while((s32[]{:T(128)}, f32[64,128]{1,0:T(8,128)S(1)}, ...), condition=%wide.region_7.8_spmd.clone, body=%wide.region_3.0_spmd.clone.sunk | while | flops 353531776 | bytes 4523659 | solution.py:42
  199.8 0.1 constant_dynamic-slice_fusion.2
  199.9 1.0 fusion.56
  201.0 1.1 fusion.57
  202.1 0.5 fusion.58
  202.5 0.7 fusion.59
  203.3 0.1 constant_dynamic-slice_fusion.2
  203.4 1.0 fusion.56
  204.5 1.1 fusion.57
  205.6 0.5 fusion.58
  206.0 0.7 fusion.59
  206.7 0.8 copy.18
  207.6 0.0 reduce-scatter.2.cloned.1.call-update
  207.6 0.0 all-reduce.4.cloned.1.call-start
  207.7 142.1 %psum.44 = f32[64,128]{1,0:T(8,128)S(1)} all-reduce(f32[64,128]{1,0:T(8,128)S(1)} %get-tuple-element.94), channel_id=1, replica_groups=mesh['row'=16,'col'=32] {'col'}, use_global_device_ids=true, to_apply=%region_9.10 | all-reduce | flops 8192 | bytes 65536 | tf_op jit(solution)/shard_map/psum | solution.py:61
  349.8 0.0 reduce-scatter.2.cloned.1.call-done
  349.8 1.6 fusion.18
  351.4 0.0 copy-start.1
  351.4 0.0 all-reduce.4.cloned.1.call-update
  351.4 0.7 copy-done.1
  352.2 0.3 fusion.22
  352.5 0.2 convolution_bitcast_fusion.4
  352.7 101.5 %all-reduce = (f32[20,256]{1,0:T(8,128)}, f32[256]{0:T(256)}) all-reduce(f32[20,256]{1,0:T(8,128)S(1)} %convolution_bitcast_fusion.4, f32[256]{0:T(256)S(1)} %get-tuple-element.155), channel_id=1, replica_groups=mesh['row'=16,'col'=32] {'row','col'}, use_global_device_ids=true, to_apply=%region_10.11 | all-reduce | flops 5376 | bytes 43008 | tf_op jit(solution)/shard_map/psum | solution.py:80
  454.2 159.8 %all-reduce.4.cloned.1.call-done = f32[256,64]{0,1:T(8,128)} async-done(((f32[256,64]{0,1:T(8,128)}), f32[256,64]{0,1:T(8,128)}) %all-reduce.4.cloned.1.call-update) | async-done | bytes 65552 | tf_op jit(solution)/shard_map/psum | solution.py:80
  614.1 1.5 copy.38
  (7 shorter events, 0.1 us)
Async XLA Ops:
  7.2 3.0 copy-start
  7.2 2.0 copy-start.5
  7.2 342.6 %reduce-scatter.2.cloned.1.call-start = ((), (), s32[]{:S(2)}) async-start(), calls=%async_computation.1 | async-start | bytes 557056 | tf_op jit(solution)/shard_map/reduce_scatter | solution.py:76
  7.3 0.7 copy-start.7
  7.3 1.9 copy-start.3
  9.2 0.7 copy-start.2
  9.2 0.7 copy-start.6
  139.9 0.7 copy-start.4
  207.6 406.5 %all-reduce.4.cloned.1.call-start = ((), (), s32[]{:S(2)}) async-start(), calls=%async_computation.2 | async-start | bytes 131072 | tf_op jit(solution)/shard_map/psum | solution.py:80
  351.4 0.8 copy-start.1
Sparse Core Ops, SparseCore 0:
  207.7 75.7 reduce-scatter.1
  351.6 262.4 all-reduce.3
where the time goes:
time: 623 us; the launch traced here: 622 us
  blocking collectives  432 us (69%)
  waiting for transfers between devices  160 us (26%)
  between operations  14.8 us (2%)
  matrix products  9.29 us (1%)
    psum x1, waiting for transfers between devices, per_device(): lax.psum((terms[0], terms[1], terms[2]), ('row', 'col'))  160 us
    psum x1, blocking collectives, window_total(): return lax.psum(partial_grad, 'col')  142 us
    psum x1, blocking collectives, spread(): return lax.psum(kept, axis)  129 us
    psum x1, blocking collectives, per_device(): lax.psum((terms[0], terms[1], terms[2]), ('row', 'col'))  102 us
    all_gather x1, blocking collectives, per_device(): lax.all_gather(probes, 'row', axis=1, tiled=True)  32.7 us
    all_gather x1, blocking collectives, per_device(): lax.all_gather(features, 'row', axis=1, tiled=True)  26.2 us
  transfers between devices with their start and end apart: 2, of which 1 were waited for; matrix products, arithmetic and copies ran while one was open for 0% of the time, Pallas kernels for 0%

commit v1 on v0

v1 whole, which is shorter than its diff:
```python
import functools

import jax
import jax.numpy as jnp
from jax import lax
from jax.experimental import pallas as pl
from jax.experimental.pallas import tpu as pltpu
from jax.sharding import PartitionSpec as P

F32 = jnp.float32
BF16 = jnp.bfloat16
MESH = pl.DeviceIdType.MESH
RING = (4, 3, 5, 2, 6, 1, 7)


def parts2(value):
    high = value.astype(BF16).astype(F32)
    return high, value - high


def parts3(value):
    high = value.astype(BF16).astype(F32)
    rest = value - high
    middle = rest.astype(BF16).astype(F32)
    return high, middle, rest - middle


def rows(*pieces):
    return jnp.concatenate(pieces, axis=0)


def lanes(*pieces):
    return jnp.concatenate(pieces, axis=1)


def low(value):
    return value.astype(BF16)


def nn(left, right):
    return lax.dot_general(left, right, (((1,), (0,)), ((), ())), preferred_element_type=F32)


def nt(left, right):
    return lax.dot_general(left, right, (((1,), (1,)), ((), ())), preferred_element_type=F32)


def first_layer(w_in, bias):
    at = lax.broadcasted_iota(jnp.int32, (24, w_in.shape[1]), 0)
    full = rows(w_in, jnp.zeros((4, w_in.shape[1]), F32))
    full = jnp.where(at == 20, bias, full)
    h, m, l = parts3(full)
    return low(rows(h, m, h, m, h, l).T)


def second_layer(w_out):
    both = rows(*parts2(w_out))
    turned = both.T
    return low(both), low(lanes(turned, turned))


def hidden_of(first, inputs):
    h, m, l = parts3(inputs)
    return jnp.tanh(nn(first, low(rows(h, h, m, m, l, h))))


def features_of(forward, hid_h, hid_l):
    four = nn(forward, hid_h) + nn(forward, hid_l)
    return four[0:64] + four[64:128]


def ones_row(width):
    at = lax.broadcasted_iota(jnp.int32, (16, width), 0)
    return jnp.where(at == 0, 1.0, 0.0)


def stack_of(feat):
    h, l = parts2(feat)
    return low(rows(h, l, ones_row(feat.shape[1])))


def weighted(acc, own):
    return acc[0:64] + acc[64:128] - own * acc[128:129]


def backprop(back, total, hidden, hid_h, hid_l, inputs):
    h, l = parts2(total)
    grad_hidden = nn(back, low(rows(h, h, l, l)))
    grad_pre = grad_hidden * (1.0 - hidden * hidden)
    pre_h, pre_l = parts2(grad_pre)
    p_h, p_l = parts2(inputs)
    left = low(rows(p_h, p_l))
    below = nt(left, low(pre_h)) + nt(left, low(pre_l))
    both = low(rows(h, l))
    above = nt(both, hid_h) + nt(both, hid_l)
    return above[0:64] + above[64:128], below[0:24] + below[24:48]


def window_sides(feat, solved):
    h, m, l = parts3(feat)
    one = rows(h, m).T
    two = rows(h, l).T
    cross_left = low(lanes(one, one, two))
    s_h, s_l = parts2(solved)
    vec_left = low(rows(s_h, s_l, s_h, s_l).T)
    half = 0.5 * jnp.sum(feat * feat, axis=0, keepdims=True)
    half = jnp.broadcast_to(half, (128, feat.shape[1])).T
    return cross_left, vec_left, lanes(half, half)


def cross_right(feat):
    h, m, l = parts3(feat)
    return low(rows(h, h, m, m, l, h))


def vec_right(vec):
    h, l = parts2(vec)
    return low(rows(h, h, l, l))


def pack(block):
    spot = lax.broadcasted_iota(jnp.int32, (16, 128), 1) // 32
    out = []
    for q in range(4):
        piece = jnp.zeros((16, 128), F32)
        for g in range(4):
            slab = block[16 * g : 16 * g + 16]
            turned = slab if g == q else pltpu.roll(slab, (32 * (g - q)) % 128, 1)
            piece = jnp.where(spot == g, turned, piece)
        out.append(piece)
    return out


def unpack(pieces):
    spot = lax.broadcasted_iota(jnp.int32, (16, 128), 1) // 32
    tiles = []
    for t in range(2):
        slabs = []
        for g in range(4):
            slab = jnp.zeros((16, 128), F32)
            for s in range(4):
                piece = pieces[4 * t + s]
                turned = piece if s == g else pltpu.roll(piece, (32 * (s - g)) % 128, 1)
                slab = jnp.where(spot == s, turned, slab)
            slabs.append(slab)
        tiles.append(rows(*slabs))
    return lanes(*tiles)


def kernel(
    protocols, w_in, b_in, w_out, solved, probes, blocks,
    col_out, in_out, bias_out, out_out,
    cols, win_b, bias_b, wout_b, sol, packed, quarter, ybuf, zbuf,
    hid_f, hid_hi, hid_lo, feat_b, stack_b, cross_b, vec_b,
    colp, colr, grads, scattered, zsum, ysum, gathered,
    local_sem, qs, qr, cs, cr, ys, yr, zs, zr, ps, pr, gs, gr, zs2, zr2, ys2, yr2, as_, ar,
):
    row = lax.axis_index("row")
    col = lax.axis_index("col")
    x_lo, z = row // 8, row % 8
    y, x_hi, core = col // 4, (col // 2) % 2, col % 2
    me = x_hi * 4 + x_lo * 2 + core
    mine = x_hi * 2 + core

    def device(a, b, c, d, e):
        return (b * 8 + d, c * 4 + a * 2 + e)

    def flip(value, bit):
        return 1 - value if bit else value

    group = []
    for k in (6, 7, 4, 5, 2, 3, 1):
        a, b, e = flip(x_hi, k & 4), flip(x_lo, k & 2), flip(core, k & 1)
        group.append((a * 4 + b * 2 + e, device(a, b, y, z, e), k))
    along_y = [((y + k) % 8, device(x_hi, x_lo, (y + k) % 8, z, core)) for k in RING]
    along_z = [((z + k) % 8, device(x_hi, x_lo, y, (z + k) % 8, core)) for k in RING]

    barrier = pltpu.get_barrier_semaphore()
    for who in [g[1] for g in group] + [p[1] for p in along_y] + [p[1] for p in along_z]:
        pl.semaphore_signal(barrier, inc=1, device_id=who, device_id_type=MESH)

    loads = [
        pltpu.make_async_copy(protocols, cols.at[me, pl.ds(0, 20)], local_sem.at[0]),
        pltpu.make_async_copy(solved, sol, local_sem.at[1]),
        pltpu.make_async_copy(probes, cols.at[me, pl.ds(24, 32)], local_sem.at[2]),
        pltpu.make_async_copy(w_in, win_b, local_sem.at[3]),
        pltpu.make_async_copy(b_in, bias_b, local_sem.at[4]),
        pltpu.make_async_copy(w_out, wout_b, local_sem.at[5]),
    ]
    for load in loads:
        load.start()
    at = lax.broadcasted_iota(jnp.int32, (4, 128), 0)
    cols[me, 20:24] = jnp.where(at == 0, 1.0, 0.0)
    for load in loads:
        load.wait()

    owner = (blocks[row] == col).astype(jnp.int32).astype(F32)
    block = rows(cols[me, 0:24], sol[...], jnp.zeros((8, 128), F32)) * owner
    for q, piece in enumerate(pack(block)):
        packed[q] = piece

    def send(source, target, ssem, rsem, who):
        copy = pltpu.make_async_remote_copy(
            src_ref=source, dst_ref=target, send_sem=ssem, recv_sem=rsem,
            device_id=who, device_id_type=MESH,
        )
        copy.start()
        return copy

    def arrive(target, ssem, rsem, who):
        pltpu.make_async_remote_copy(
            src_ref=target, dst_ref=target, send_sem=ssem, recv_sem=rsem,
            device_id=who, device_id_type=MESH,
        ).wait_recv()

    pl.semaphore_wait(barrier, 21)
    started = []

    fours = [(g, who, k) for g, who, k in group if not k & 2]
    for i, (g, who, k) in enumerate(fours):
        q = (g // 4) * 2 + g % 2
        started.append(send(packed.at[q], quarter.at[mine], qs.at[i], qr.at[mine], who))
    for i, (g, who, k) in enumerate(group):
        started.append(send(cols.at[me], cols.at[me], cs.at[i], cr.at[me], who))

    first = first_layer(win_b[...], bias_b[...])
    forward, back = second_layer(wout_b[...])

    quarter[mine] = packed[mine]
    for i, (g, who, k) in enumerate(fours):
        q = (g // 4) * 2 + g % 2
        arrive(quarter.at[q], qs.at[i], qr.at[q], who)
    ybuf[y] = quarter[0] + quarter[1] + quarter[2] + quarter[3]
    for i, (s, who) in enumerate(along_y):
        started.append(send(ybuf.at[y], ybuf.at[y], ys.at[i], yr.at[y], who))

    def columns(chunk):
        spread = lanes(cols[2 * chunk], cols[2 * chunk + 1])
        inputs, vec = spread[0:24], spread[24:56]
        hidden = hidden_of(first, inputs)
        h, l = parts2(hidden)
        h, l = low(h), low(l)
        feat = features_of(forward, h, l)
        hid_f[chunk] = hidden
        hid_hi[chunk] = h
        hid_lo[chunk] = l
        feat_b[chunk] = feat
        stack_b[chunk] = stack_of(feat)
        cross_b[chunk] = cross_right(feat)
        vec_b[chunk] = vec_right(vec)

    for i, (g, who, k) in enumerate(group):
        arrive(cols.at[g], cs.at[i], cr.at[g], who)
    columns(0)
    columns(1)

    for i, (s, who) in enumerate(along_y):
        arrive(ybuf.at[s], ys.at[i], yr.at[s], who)
    merged = ybuf[0]
    for s in range(1, 8):
        merged = merged + ybuf[s]
    zbuf[z] = merged
    for i, (s, who) in enumerate(along_z):
        started.append(send(zbuf.at[z], zbuf.at[z], zs.at[i], zr.at[z], who))

    columns(2)
    columns(3)

    for i, (s, who) in enumerate(along_z):
        arrive(zbuf.at[s], zs.at[i], zr.at[s], who)
    window = unpack([zbuf[s] for s in range(8)])
    win_in = window[0:24]
    win_hidden = hidden_of(first, win_in)
    win_h, win_l = parts2(win_hidden)
    win_h, win_l = low(win_h), low(win_l)
    win_feat = features_of(forward, win_h, win_l)
    cross_left, vec_left, half_win = window_sides(win_feat, window[24:56])
    win_stack = stack_of(win_feat)

    win_acc = jnp.zeros((144, 256), F32)
    above = jnp.zeros((64, 256), F32)
    below = jnp.zeros((24, 256), F32)
    for c in range(4):
        feat = feat_b[c]
        half = 0.5 * jnp.sum(feat * feat, axis=0, keepdims=True)
        kern = jnp.exp(nn(cross_left, cross_b[c]) - half_win - half)
        weigh = kern * nn(vec_left, vec_b[c])
        w_h, w_l = parts2(weigh)
        w_h, w_l = low(w_h), low(w_l)
        part = weighted(nn(win_stack, w_h) + nn(win_stack, w_l), feat)
        colp[2 * c] = part[:, 0:128]
        colp[2 * c + 1] = part[:, 128:256]
        win_acc = win_acc + nt(stack_b[c], w_h) + nt(stack_b[c], w_l)
        inputs = lanes(cols[2 * c, 0:24], cols[2 * c + 1, 0:24])
        more = backprop(back, part, hid_f[c], hid_hi[c], hid_lo[c], inputs)
        above = above + more[0]
        below = below + more[1]
    win_part = weighted(win_acc, win_feat)
    more = backprop(back, win_part, win_hidden, win_h, win_l, win_in)
    above = above + more[0]
    below = below + more[1]

    for p in range(8):
        grads[p, 0:8] = above[8 * p : 8 * p + 8, 0:128]
        grads[p, 8:16] = above[8 * p : 8 * p + 8, 128:256]
        if p < 6:
            t, s = p // 2, p % 2
            grads[p, 16:24] = below[8 * t : 8 * t + 8, 128 * s : 128 * s + 128]
        else:
            grads[p, 16:24] = jnp.zeros((8, 128), F32)

    for i, (g, who, k) in enumerate(group):
        started.append(send(grads.at[g], scattered.at[me], gs.at[i], gr.at[me], who))
    for i, (g, who, k) in enumerate(group):
        started.append(send(colp.at[g], colr.at[me], ps.at[i], pr.at[me], who))
    scattered[me] = grads[me]
    for i, (g, who, k) in enumerate(group):
        arrive(scattered.at[g], gs.at[i], gr.at[g], who)
    total = scattered[0]
    for s in range(1, 8):
        total = total + scattered[s]
    zsum[z] = total
    for i, (s, who) in enumerate(along_z):
        started.append(send(zsum.at[z], zsum.at[z], zs2.at[i], zr2.at[z], who))

    colr[me] = colp[me]
    for i, (g, who, k) in enumerate(group):
        arrive(colr.at[g], ps.at[i], pr.at[g], who)
    col_grad = colr[0]
    for s in range(1, 8):
        col_grad = col_grad + colr[s]
    col_out[...] = col_grad

    for i, (s, who) in enumerate(along_z):
        arrive(zsum.at[s], zs2.at[i], zr2.at[s], who)
    total = zsum[0]
    for s in range(1, 8):
        total = total + zsum[s]
    ysum[y] = total
    for i, (s, who) in enumerate(along_y):
        started.append(send(ysum.at[y], ysum.at[y], ys2.at[i], yr2.at[y], who))
    for i, (s, who) in enumerate(along_y):
        arrive(ysum.at[s], ys2.at[i], yr2.at[s], who)
    total = ysum[0]
    for s in range(1, 8):
        total = total + ysum[s]
    gathered[me] = total
    for i, (g, who, k) in enumerate(group):
        started.append(send(gathered.at[me], gathered.at[me], as_.at[i], ar.at[me], who))
    for i, (g, who, k) in enumerate(group):
        arrive(gathered.at[g], as_.at[i], ar.at[g], who)

    for p in range(8):
        out_out[8 * p : 8 * p + 8] = lanes(gathered[p, 0:8], gathered[p, 8:16])
    below = [lanes(gathered[2 * t, 16:24], gathered[2 * t + 1, 16:24]) for t in range(3)]
    in_out[0:16] = rows(*below[0:2])
    in_out[16:20] = below[2][0:4]
    bias_out[...] = below[2][4:5]
    for copy in started:
        copy.wait_send()


def per_device(protocols, w_in, b_in, w_out, solved, probes, window_blocks):
    anywhere = pl.BlockSpec(memory_space=pl.ANY)
    vmem = pl.BlockSpec(memory_space=pltpu.VMEM)
    dma = pltpu.SemaphoreType.DMA
    col_grad, grad_in, grad_bias, grad_out = pl.pallas_call(
        kernel,
        out_shape=(
            jax.ShapeDtypeStruct((64, 128), F32),
            jax.ShapeDtypeStruct((20, 256), F32),
            jax.ShapeDtypeStruct((1, 256), F32),
            jax.ShapeDtypeStruct((64, 256), F32),
        ),
        in_specs=[anywhere] * 6 + [pl.BlockSpec(memory_space=pltpu.SMEM)],
        out_specs=(vmem, vmem, vmem, vmem),
        scratch_shapes=[
            pltpu.VMEM((8, 56, 128), F32),
            pltpu.VMEM((20, 256), F32),
            pltpu.VMEM((1, 256), F32),
            pltpu.VMEM((64, 256), F32),
            pltpu.VMEM((32, 128), F32),
            pltpu.VMEM((4, 16, 128), F32),
            pltpu.VMEM((4, 16, 128), F32),
            pltpu.VMEM((8, 16, 128), F32),
            pltpu.VMEM((8, 16, 128), F32),
            pltpu.VMEM((4, 256, 256), F32),
            pltpu.VMEM((4, 256, 256), BF16),
            pltpu.VMEM((4, 256, 256), BF16),
            pltpu.VMEM((4, 64, 256), F32),
            pltpu.VMEM((4, 144, 256), BF16),
            pltpu.VMEM((4, 384, 256), BF16),
            pltpu.VMEM((4, 128, 256), BF16),
            pltpu.VMEM((8, 64, 128), F32),
            pltpu.VMEM((8, 64, 128), F32),
            pltpu.VMEM((8, 24, 128), F32),
            pltpu.VMEM((8, 24, 128), F32),
            pltpu.VMEM((8, 24, 128), F32),
            pltpu.VMEM((8, 24, 128), F32),
            pltpu.VMEM((8, 24, 128), F32),
            dma((6,)),
            dma((3,)), dma((4,)),
            dma((7,)), dma((8,)),
            dma((7,)), dma((8,)),
            dma((7,)), dma((8,)),
            dma((7,)), dma((8,)),
            dma((7,)), dma((8,)),
            dma((7,)), dma((8,)),
            dma((7,)), dma((8,)),
            dma((7,)), dma((8,)),
        ],
        compiler_params=pltpu.CompilerParams(collective_id=0, has_side_effects=True),
    )(protocols, w_in, b_in.reshape(1, 256), w_out.T, solved, probes, window_blocks)
    return col_grad, grad_in, grad_bias.reshape(256), grad_out.T


def solution(mesh):
    split = P(None, ("row", "col"))
    return jax.shard_map(
        per_device,
        mesh=mesh,
        in_specs=(split, P(), P(), P(), split, split, P()),
        out_specs=(split, P(), P(), P()),
        check_vma=False,
    )
```

time: 623 us -> 57.3 us (0.09)
  blocking collectives: 432 us -> 0 us
  waiting for transfers between devices: 160 us -> 0 us
  Pallas kernels: 0 us -> 52.4 us
  between operations: 14.8 us -> 0.65 us
  matrix products: 9.29 us -> 0 us
    psum x3 -> x0, blocking collectives: 373 us -> none  [the longest x1 142 us: window_total(): return lax.psum(partial_grad, 'col')]
    psum x1 -> x0, waiting for transfers between devices: 160 us -> none  [per_device(): lax.psum((terms[0], terms[1], terms[2]), ('row', 'col'))]
    all_gather x2 -> x0, blocking collectives: 58.9 us -> none  [the longest x1 32.7 us: per_device(): lax.all_gather(probes, 'row', axis=1, tiled=True)]
    pallas_call x0 -> x1, Pallas kernels: none -> 52.4 us  [per_device(): pl.pallas_call(kernel, out_shape=(jax.ShapeDtypeStruct((64, 128), F32), j...]
    dot_general x13 -> x0, matrix products: 9.29 us -> none  [the longest x2 2.17 us: tile_pass(): jnp.einsum('qi,qj->ij', first_vec, second_vec, precision=HIGHEST) * kern]
  transfers between devices with their start and end apart: 2 -> 0, of which waited for: 1 -> 0; matrix products, arithmetic and copies ran while one was open for 0% -> 0% of each run, Pallas kernels for 0% -> 0%
where the time goes in v1:
time: 57.3 us; the launch traced here: 57 us
  Pallas kernels  52.4 us (91%)
  local copies, waits for them, and re-layouts  3.95 us (7%)
  between operations  0.65 us (1%)
    pallas_call x1, Pallas kernels, per_device(): pl.pallas_call(kernel, out_shape=(jax.ShapeDtypeStruct((64, 128), F32), j...  52.4 us
    unnamed x8, local copies, waits for them, and re-layouts  3.95 us

profile of v1, /device:TPU:1, one launch (start us, length us, event | category | flops | bytes accessed | tf_op | source)
XLA Modules:
  0.0 57.0 jit_solution(1170120424719882185)
XLA Ops:
  0.6 52.4 %shard_map.102 = (f32[64,128]{1,0:T(8,128)}, f32[20,256]{1,0:T(8,128)}, f32[1,256]{1,0:T(1,128)}, f32[64,256]{1,0:T(8,128)}) custom-call(f32[20,128]{1,0:T(8,128)} %protocols.1, f32[20,256]{1,0:T(8,128)} %w_in.1, f32[1,256]{1,0:T(1,128)} %bitcast.6, f32[64,256]{1,0:T(8,128)} %bitcast.4, f32[32,128]{1,0:T(8,128)} %solved.1, f32[32,128]{1,0:T(8,128)} %probes.1, ...), custom_call_target="tpu_custom_call" | custom-call | tf_op jit(solution)/shard_map/pallas_call | solution.py:367
  53.0 0.0 copy-start
  53.0 1.4 %copy.15 = f32[64,128]{1,0:T(8,128)} copy(f32[64,128]{1,0:T(8,128)} %get-tuple-element.16) | data formatting | bytes 65536
  54.4 0.0 copy-start.1
  54.4 1.3 %copy.16 = f32[20,256]{1,0:T(8,128)} copy(f32[20,256]{1,0:T(8,128)} %get-tuple-element.17) | data formatting | bytes 40960
  55.8 0.0 copy-done.1
  55.8 0.6 copy.17
  56.3 0.0 copy-done
  56.3 0.6 %copy.18 = f32[256,64]{0,1:T(8,128)} copy(f32[256,64]{0,1:T(8,128)S(1)} %bitcast.5) | data formatting | bytes 131072
Async XLA Ops:
  53.0 3.3 %copy-start = (f32[64,256]{1,0:T(8,128)S(1)}, f32[64,256]{1,0:T(8,128)}, u32[]{:S(2)}) copy-start(f32[64,256]{1,0:T(8,128)} %get-tuple-element.11) | copy-start | bytes 196612
  54.4 1.4 %copy-start.1 = (f32[1,256]{1,0:T(1,128)S(1)}, f32[1,256]{1,0:T(1,128)}, u32[]{:S(2)}) copy-start(f32[1,256]{1,0:T(1,128)} %get-tuple-element.10) | copy-start | bytes 3076

commit v2 on v1

v2 whole, which is shorter than its diff:
```python
import functools

import jax
import jax.numpy as jnp
from jax import lax
from jax.experimental import pallas as pl
from jax.experimental.pallas import tpu as pltpu
from jax.sharding import PartitionSpec as P

F32 = jnp.float32
BF16 = jnp.bfloat16
MESH = pl.DeviceIdType.MESH
RING = (4, 3, 5, 2, 6, 1, 7)


def parts2(value):
    high = value.astype(BF16).astype(F32)
    return high, value - high


def parts3(value):
    high = value.astype(BF16).astype(F32)
    rest = value - high
    middle = rest.astype(BF16).astype(F32)
    return high, middle, rest - middle


def rows(*pieces):
    return jnp.concatenate(pieces, axis=0)


def lanes(*pieces):
    return jnp.concatenate(pieces, axis=1)


def low(value):
    return value.astype(BF16)


def nn(left, right):
    return lax.dot_general(left, right, (((1,), (0,)), ((), ())), preferred_element_type=F32)


def nt(left, right):
    return lax.dot_general(left, right, (((1,), (1,)), ((), ())), preferred_element_type=F32)


def first_layer(w_in, bias):
    at = lax.broadcasted_iota(jnp.int32, (24, w_in.shape[1]), 0)
    full = rows(w_in, jnp.zeros((4, w_in.shape[1]), F32))
    full = jnp.where(at == 20, bias, full)
    h, m, l = parts3(full)
    return low(rows(h, m, h, m, h, l).T)


def second_layer(w_out):
    both = rows(*parts2(w_out))
    turned = both.T
    return low(both), low(lanes(turned, turned))


def hidden_of(first, inputs):
    h, m, l = parts3(inputs)
    return jnp.tanh(nn(first, low(rows(h, h, m, m, l, h))))


def features_of(forward, hid_h, hid_l):
    four = nn(forward, hid_h) + nn(forward, hid_l)
    return four[0:64] + four[64:128]


def ones_row(width):
    at = lax.broadcasted_iota(jnp.int32, (16, width), 0)
    return jnp.where(at == 0, 1.0, 0.0)


def stack_of(feat):
    h, l = parts2(feat)
    return low(rows(h, l, ones_row(feat.shape[1])))


def weighted(acc, own):
    return acc[0:64] + acc[64:128] - own * acc[128:129]


def column_sides(feat, vec):
    h, m, l = parts3(feat)
    one = rows(h, m).T
    two = rows(h, l).T
    v_h, v_l = parts2(vec)
    half = 0.5 * jnp.sum(feat * feat, axis=0, keepdims=True)
    half = jnp.broadcast_to(half, (128, feat.shape[1])).T
    return low(lanes(one, one, two)), low(rows(v_h, v_l, v_h, v_l).T), half


def cross_right(feat):
    h, m, l = parts3(feat)
    return low(rows(h, h, m, m, l, h))


def vec_right(vec):
    h, l = parts2(vec)
    return low(rows(h, h, l, l))


def pack(block):
    spot = lax.broadcasted_iota(jnp.int32, (16, 128), 1) // 32
    out = []
    for q in range(4):
        piece = jnp.zeros((16, 128), F32)
        for g in range(4):
            slab = block[16 * g : 16 * g + 16]
            turned = slab if g == q else pltpu.roll(slab, (32 * (g - q)) % 128, 1)
            piece = jnp.where(spot == g, turned, piece)
        out.append(piece)
    return out


def unpack(pieces):
    spot = lax.broadcasted_iota(jnp.int32, (16, 128), 1) // 32
    tiles = []
    for t in range(2):
        slabs = []
        for g in range(4):
            slab = jnp.zeros((16, 128), F32)
            for s in range(4):
                piece = pieces[4 * t + s]
                turned = piece if s == g else pltpu.roll(piece, (32 * (s - g)) % 128, 1)
                slab = jnp.where(spot == s, turned, slab)
            slabs.append(slab)
        tiles.append(rows(*slabs))
    return lanes(*tiles)


def kernel(
    protocols, w_in, b_in, w_out, solved, probes, blocks,
    col_out, in_out, bias_out, out_out,
    owners, cols, win_b, bias_b, wout_b, sol, packed, quarter, ybuf, zbuf,
    slope_b, hid_hi, hid_lo, feat_b, stack_b, cross_b, vec_b, half_b,
    colp, colr, grads, grads_x, grads_z, grads_y, grads_g,
    load_sem, known, quarter_sem, cols_sem, y_sem, z_sem, colr_sem,
    sums_x_sem, sums_z_sem, sums_y_sem, sums_g_sem,
):
    row = lax.axis_index("row")
    col = lax.axis_index("col")
    x_lo, z = row // 8, row % 8
    y, x_hi, core = col // 4, (col // 2) % 2, col % 2
    me = x_hi * 4 + x_lo * 2 + core
    mine = x_hi * 2 + core

    def device(a, b, c, d, e):
        return (b * 8 + d, c * 4 + a * 2 + e)

    def flip(value, bit):
        return 1 - value if bit else value

    loads = [
        pltpu.make_async_copy(protocols, cols.at[me, pl.ds(0, 20)], load_sem.at[0]),
        pltpu.make_async_copy(solved, sol, load_sem.at[1]),
        pltpu.make_async_copy(blocks, owners, load_sem.at[2]),
        pltpu.make_async_copy(probes, cols.at[me, pl.ds(24, 32)], load_sem.at[3]),
        pltpu.make_async_copy(w_in, win_b, load_sem.at[4]),
        pltpu.make_async_copy(b_in, bias_b, load_sem.at[5]),
        pltpu.make_async_copy(w_out, wout_b, load_sem.at[6]),
    ]
    for load in loads:
        load.start()

    group = []
    for k in (6, 7, 4, 5, 2, 3, 1):
        a, b, e = flip(x_hi, k & 4), flip(x_lo, k & 2), flip(core, k & 1)
        group.append((a * 4 + b * 2 + e, device(a, b, y, z, e), None if k & 2 else a * 2 + e))
    fours = [(q, who) for g, who, q in group if q is not None]
    group = [(g, who) for g, who, q in group]
    along_y = [((y + k) % 8, device(x_hi, x_lo, (y + k) % 8, z, core)) for k in RING]
    along_z = [((z + k) % 8, device(x_hi, x_lo, y, (z + k) % 8, core)) for k in RING]

    def at_distance(k):
        ends = [RING.index(k), RING.index(8 - k)]
        return [along_y[i][1] for i in ends] + [along_z[i][1] for i in ends]

    def greet(sem, devices):
        for who in devices:
            pl.semaphore_signal(sem, inc=1, device_id=who, device_id_type=MESH)

    barrier = pltpu.get_barrier_semaphore()
    greet(barrier, [who for g, who in group] + at_distance(1))

    finish = []

    def send(pairs, buffer, sems, here):
        for source, who in pairs:
            pltpu.make_async_remote_copy(
                src_ref=source, dst_ref=buffer.at[here], send_sem=sems.at[0], recv_sem=sems.at[1],
                device_id=who, device_id_type=MESH,
            ).start()
        count = len(pairs)
        some = buffer.at[pl.ds(0, count)]
        every = pltpu.make_async_remote_copy(
            src_ref=some, dst_ref=some, send_sem=sems.at[0], recv_sem=sems.at[1],
            device_id=pairs[0][1], device_id_type=MESH,
        )
        finish.append(every)
        return every.wait_recv

    def spread(buffer, sems, here, partners):
        return send([(buffer.at[here], who) for s, who in partners], buffer, sems, here)

    def scatter(pieces, buffer, sems, here, partners):
        return send([(pieces.at[s], who) for s, who in partners], buffer, sems, here)

    def summed(buffer, count=8):
        total = buffer[0]
        for s in range(1, count):
            total = total + buffer[s]
        return total

    at = lax.broadcasted_iota(jnp.int32, (4, 128), 0)
    cols[me, 20:24] = jnp.where(at == 0, 1.0, 0.0)
    for load in loads[0:3]:
        load.wait()

    owner = (owners[row] == col).astype(jnp.int32).astype(F32)
    block = rows(cols[me, 0:24], sol[...], jnp.zeros((8, 128), F32)) * owner
    for q, piece in enumerate(pack(block)):
        packed[q] = piece

    pl.semaphore_wait(barrier, 11)
    greet(known.at[0], at_distance(1))

    quarters_in = scatter(packed, quarter, quarter_sem, mine, fours)

    quarter[mine] = packed[mine]
    for load in loads[3:]:
        load.wait()
    first = first_layer(win_b[...], bias_b[...])
    forward, back = second_layer(wout_b[...])
    pl.semaphore_wait(known.at[0], 4)
    greet(known.at[1], at_distance(2))

    quarters_in()
    ybuf[y] = summed(quarter, 4)
    pl.semaphore_wait(known.at[1], 4)
    y_in = spread(ybuf, y_sem, y, along_y)
    cols_in = spread(cols, cols_sem, me, group)

    def columns(chunk):
        both = lanes(cols[2 * chunk], cols[2 * chunk + 1])
        inputs, vec = both[0:24], both[24:56]
        hidden = hidden_of(first, inputs)
        h, l = parts2(hidden)
        h, l = low(h), low(l)
        feat = features_of(forward, h, l)
        slope_b[chunk] = 1.0 - hidden * hidden
        hid_hi[chunk] = h
        hid_lo[chunk] = l
        feat_b[chunk] = feat
        stack_b[chunk] = stack_of(feat)
        cross_b[chunk], vec_b[chunk], half_b[chunk] = column_sides(feat, vec)

    y_in()
    zbuf[z] = summed(ybuf)
    z_in = spread(zbuf, z_sem, z, along_z)

    cols_in()
    for chunk in range(4):
        columns(chunk)

    z_in()

    window = unpack([zbuf[s] for s in range(8)])
    win_in = window[0:24]
    win_hidden = hidden_of(first, win_in)
    win_h, win_l = parts2(win_hidden)
    win_h, win_l = low(win_h), low(win_l)
    win_feat = features_of(forward, win_h, win_l)
    win_cross, win_vec = cross_right(win_feat), vec_right(window[24:56])
    win_half = 0.5 * jnp.sum(win_feat * win_feat, axis=0, keepdims=True)
    win_stack = stack_of(win_feat)

    weights = []
    for c in range(4):
        half = lanes(half_b[c], half_b[c])
        kern = jnp.exp(nn(cross_b[c], win_cross) - half - win_half)
        w_h, w_l = parts2(kern * nn(vec_b[c], win_vec))
        weights.append((low(w_h), low(w_l)))
    win_h_acc = win_l_acc = jnp.zeros((144, 256), F32)
    totals = []
    for c, (w_h, w_l) in enumerate(weights):
        part = weighted(nt(win_stack, w_h) + nt(win_stack, w_l), feat_b[c])
        win_h_acc = win_h_acc + nn(stack_b[c], w_h)
        win_l_acc = win_l_acc + nn(stack_b[c], w_l)
        colp[2 * c] = part[:, 0:128]
        colp[2 * c + 1] = part[:, 128:256]
        totals.append(part)
    totals.append(weighted(win_h_acc + win_l_acc, win_feat))

    above_h = above_l = jnp.zeros((128, 256), F32)
    below_h = below_l = jnp.zeros((48, 256), F32)
    slopes = []
    for c, part in enumerate(totals):
        part_h, part_l = parts2(part)
        both = low(rows(part_h, part_l))
        last = c == 4
        slope = 1.0 - win_hidden * win_hidden if last else slope_b[c]
        four = rows(both[0:64], both[0:64], both[64:128], both[64:128])
        slopes.append(parts2(nn(back, four) * slope))
        above_h = above_h + nt(both, win_h if last else hid_hi[c])
        above_l = above_l + nt(both, win_l if last else hid_lo[c])
    for c, (pre_h, pre_l) in enumerate(slopes):
        inputs = win_in if c == 4 else lanes(cols[2 * c, 0:24], cols[2 * c + 1, 0:24])
        left = low(rows(*parts2(inputs)))
        below_h = below_h + nt(left, low(pre_h))
        below_l = below_l + nt(left, low(pre_l))
    above, below = above_h + above_l, below_h + below_l
    above = above[0:64] + above[64:128]
    below = below[0:24] + below[24:48]
    for p in range(8):
        grads[p, 0:8] = above[8 * p : 8 * p + 8, 0:128]
        grads[p, 8:16] = above[8 * p : 8 * p + 8, 128:256]
        if p < 6:
            t, s = p // 2, p % 2
            grads[p, 16:24] = below[8 * t : 8 * t + 8, 128 * s : 128 * s + 128]
        else:
            grads[p, 16:24] = jnp.zeros((8, 128), F32)

    x_in = scatter(grads, grads_x, sums_x_sem, me, group)
    grads_x[me] = grads[me]
    x_in()
    grads_z[z] = summed(grads_x)

    z_in = spread(grads_z, sums_z_sem, z, along_z)
    colr_in = scatter(colp, colr, colr_sem, me, group)
    colr[me] = colp[me]
    z_in()
    grads_y[y] = summed(grads_z)

    y_in = spread(grads_y, sums_y_sem, y, along_y)
    colr_in()
    col_out[...] = summed(colr)
    y_in()
    grads_g[me] = summed(grads_y)

    g_in = spread(grads_g, sums_g_sem, me, group)
    for every in finish[:-1]:
        every.wait_send()
    g_in()

    for p in range(8):
        out_out[8 * p : 8 * p + 8] = lanes(grads_g[p, 0:8], grads_g[p, 8:16])
    below = [lanes(grads_g[2 * t, 16:24], grads_g[2 * t + 1, 16:24]) for t in range(3)]
    in_out[0:16] = rows(*below[0:2])
    in_out[16:20] = below[2][0:4]
    bias_out[...] = below[2][4:5]
    finish[-1].wait_send()


SHAPES = ((64, 128), (20, 256), (1, 256), (64, 256))


def write_out(a, b, c, d, a_out, b_out, c_out, d_out, sems):
    pairs = ((a, a_out), (b, b_out), (c, c_out), (d, d_out))
    copies = [pltpu.make_async_copy(s, t, sems.at[i]) for i, (s, t) in enumerate(pairs)]
    for copy in copies:
        copy.start()
    for copy in copies:
        copy.wait()


def per_device(protocols, w_in, b_in, w_out, solved, probes, window_blocks):
    anywhere = pl.BlockSpec(memory_space=pl.ANY)
    vmem = pl.BlockSpec(memory_space=pltpu.VMEM)
    dma = pltpu.SemaphoreType.DMA
    results = pl.pallas_call(
        kernel,
        out_shape=tuple(pltpu.VMEM(shape, F32) for shape in SHAPES),
        in_specs=[anywhere] * 7,
        out_specs=(vmem, vmem, vmem, vmem),
        scratch_shapes=[
            pltpu.SMEM((16,), jnp.int32),
            pltpu.VMEM((8, 56, 128), F32),
            pltpu.VMEM((20, 256), F32),
            pltpu.VMEM((1, 256), F32),
            pltpu.VMEM((64, 256), F32),
            pltpu.VMEM((32, 128), F32),
            pltpu.VMEM((4, 16, 128), F32),
            pltpu.VMEM((4, 16, 128), F32),
            pltpu.VMEM((8, 16, 128), F32),
            pltpu.VMEM((8, 16, 128), F32),
            pltpu.VMEM((4, 256, 256), F32),
            pltpu.VMEM((4, 256, 256), BF16),
            pltpu.VMEM((4, 256, 256), BF16),
            pltpu.VMEM((4, 64, 256), F32),
            pltpu.VMEM((4, 144, 256), BF16),
            pltpu.VMEM((4, 256, 384), BF16),
            pltpu.VMEM((4, 256, 128), BF16),
            pltpu.VMEM((4, 256, 128), F32),
            pltpu.VMEM((8, 64, 128), F32),
            pltpu.VMEM((8, 64, 128), F32),
            *[pltpu.VMEM((8, 24, 128), F32)] * 5,
            dma((7,)),
            pltpu.SemaphoreType.REGULAR((2,)),
            *[dma((2,))] * 9,
        ],
        compiler_params=pltpu.CompilerParams(collective_id=0, has_side_effects=True),
    )(protocols, w_in, b_in.reshape(1, 256), w_out.T, solved, probes, window_blocks)
    col_grad, grad_in, grad_bias, grad_out = pl.pallas_call(
        write_out,
        out_shape=tuple(jax.ShapeDtypeStruct(shape, F32) for shape in SHAPES),
        in_specs=[vmem] * 4,
        out_specs=(anywhere,) * 4,
        scratch_shapes=[dma((4,))],
    )(*[pltpu.with_memory_space_constraint(v, pltpu.VMEM) for v in results])
    return col_grad, grad_in, grad_bias.reshape(256), grad_out.T


def solution(mesh):
    split = P(None, ("row", "col"))
    return jax.shard_map(
        per_device,
        mesh=mesh,
        in_specs=(split, P(), P(), P(), split, split, P()),
        out_specs=(split, P(), P(), P()),
        check_vma=False,
    )
```

time: 57.3 us -> 48.6 us (0.85)
  Pallas kernels: 52.4 us -> 47.8 us
  local copies, waits for them, and re-layouts: 3.95 us -> 0 us
    pallas_call x1 -> x2, Pallas kernels: 52.4 us -> 47.8 us  [the longest x1 47.1 us: per_device(): pl.pallas_call(kernel, out_shape=tuple((pltpu.VMEM(shape, F32) for shape...]
    unnamed x8 -> x0, local copies, waits for them, and re-layouts: 3.95 us -> none
where the time goes in v2:
time: 48.6 us; the launch traced here: 48.4 us
  Pallas kernels  47.8 us (98%)
  between operations  0.64 us (1%)
    pallas_call x1, Pallas kernels, per_device(): pl.pallas_call(kernel, out_shape=tuple((pltpu.VMEM(shape, F32) for shape...  47.1 us

profile of v2, /device:TPU:1, one launch (start us, length us, event | category | flops | bytes accessed | tf_op | source)
XLA Modules:
  0.0 48.4 jit_solution(5743476367896490569)
XLA Ops:
  0.6 47.1 %shard_map.102 = (f32[64,128]{1,0:T(8,128)S(1)}, f32[20,256]{1,0:T(8,128)S(1)}, f32[1,256]{1,0:T(1,128)S(1)}, f32[64,256]{1,0:T(8,128)S(1)}) custom-call(f32[20,128]{1,0:T(8,128)} %protocols.1, f32[20,256]{1,0:T(8,128)} %w_in.1, f32[1,256]{1,0:T(1,128)} %bitcast.5, f32[64,256]{1,0:T(8,128)} %bitcast.4, f32[32,128]{1,0:T(8,128)} %solved.1, f32[32,128]{1,0:T(8,128)} %probes.1, ...), custom_call_target="tpu_custom_call" | custom-call | tf_op jit(solution)/shard_map/pallas_call | solution.py:374
  47.7 0.7 %shard_map.103 = (f32[64,128]{1,0:T(8,128)}, f32[20,256]{1,0:T(8,128)}, f32[1,256]{1,0:T(1,128)}, f32[64,256]{1,0:T(8,128)}) custom-call(f32[64,128]{1,0:T(8,128)S(1)} %get-tuple-element.12.a, f32[20,256]{1,0:T(8,128)S(1)} %get-tuple-element.13.b, f32[1,256]{1,0:T(1,128)S(1)} %get-tuple-element.14.c, f32[64,256]{1,0:T(8,128)S(1)} %get-tuple-element.15.d), custom_call_target="tpu_custom_call" | custom-call | tf_op jit(solution)/shard_map/pallas_call | solution.py:407
